TPU v7x, 256 devices: a whole 4x4x8 slice. The times are simulated.
256 devices in a mesh: dp: 64 (over z, x, core), tensor: 4 (over y).
Axes of the slice: x: 4, y: 4, z: 8, core: 2. Of those that a mesh axis runs over, the one named last changes fastest.
Arguments:
- hidden: bfloat16 [8192, 4096], P('dp', 'tensor'), may hold values from -6 to 6
- grad_out: bfloat16 [8192, 4096], P('dp', 'tensor'), may hold values from -0.59765625 to 0.59765625
- query_weight: bfloat16 [4096, 4096], P(None, 'tensor'), may hold values from -0.09375 to 0.09375
- key_weight: bfloat16 [768, 4096], P(None, 'tensor'), may hold values from -0.21875 to 0.21875
- value_weight: bfloat16 [768, 4096], P(None, 'tensor'), may hold values from -0.21875 to 0.21875
- out_weight: bfloat16 [4096, 4096], P('tensor', 'dp'), may hold values from -0.75 to 0.75
- neighbour_states: bfloat16 [256, 128, 768], P('dp', None, 'tensor'), may hold values from -6 to 6
- block_owner: int32 [64, 4], P('dp'), may hold values from 0 to 63, as said below
- slot_target: int32 [64, 4], P('dp'), may hold values from 0 to 63, as said below
Outputs:
- cross_out: bfloat16 [8192, 4096], P('dp', 'tensor')
- grad_hidden: bfloat16 [8192, 4096], P('dp', 'tensor')
- grad_states: bfloat16 [256, 128, 768], P('dp', None, 'tensor')
Inputs may be any that keep to these rules, and one draw needn't show every extreme that they name: block_owner[d, t] = o exactly when slot_target[o, t] = d. The blocks 2k and 2k+1 of a dp index share their holder; the difference (holder - d) modulo the dp count is the same for every d, lies in 1 to 4, and differs between k. So a dp index holds exactly 2 blocks for each of 2 other indices. `slot_target`: the inverse map of block_owner, as stated there.
All inputs are finite; a program needn't handle non-finite values.
Results may differ from a plain program's by a relative error of at most 0.012.
Values may be sent and summed in bfloat16 or wider, within the bound.
No kernel may reach another device: no remote copies, remote signals or barrier semaphores. Data moves between devices by JAX's collectives and lax.ppermute only.
A program may use at most 128 MiB of HBM per device.

v0:
```python
import math
import jax
import jax.numpy as jnp
from jax import lax
from jax.sharding import PartitionSpec as P

HEADS = 32
SPAN = 64
K_NB = 2
CAP = 2
WINDOW = 4


def side_by_side(arrays, axis, dim, along):
    both = jnp.concatenate(arrays, axis=along)
    out, at, gathered = (lax.all_gather(both, axis, axis=dim, tiled=True), 0, [])
    for a in arrays:
        gathered.append(lax.slice_in_dim(out, at, at + a.shape[along], axis=along))
        at += a.shape[along]
    return tuple(gathered)


def shifted(x, axis, by):
    devices = lax.axis_size(axis)
    return lax.ppermute(x, axis, [(i, (i + by) % devices) for i in range(devices)])


def joined_along(tiles, dim):
    dims = list(tiles.shape[1:])
    dims[dim] *= tiles.shape[0]
    return jnp.moveaxis(tiles, 0, dim).reshape(dims)


def from_everyone(x, axis):
    copies = jnp.broadcast_to(x, (lax.axis_size(axis), *x.shape))
    return lax.all_to_all(copies, axis, split_axis=0, concat_axis=0, tiled=True)


def gathered_copies(x, axis, dim):
    return joined_along(from_everyone(x, axis), dim)


def split_up(x, dim, devices):
    dims = x.shape
    tiles = x.reshape(*dims[:dim], devices, dims[dim] // devices, *dims[dim + 1 :])
    return jnp.moveaxis(tiles, dim, 0)


def summed_on_arrival(x, axis, dim):
    tiles = split_up(x, dim, lax.axis_size(axis))
    arrived = lax.all_to_all(tiles, axis, split_axis=0, concat_axis=0, tiled=True)
    return arrived.astype(jnp.float32).sum(axis=0)


def sent_together(arrays, axis, dim, along):
    ends, at = ([], 0)
    for a in arrays[:-1]:
        at += a.shape[along]
        ends.append(at)
    both = jnp.concatenate(arrays, axis=along)
    return tuple(jnp.split(summed_on_arrival(both, axis, dim), ends, axis=along))


def contract_last(left, right):
    return lax.dot_general(
        left, right, (((1,), (1,)), ((), ())), preferred_element_type=jnp.float32
    )


def contract_first(left, right):
    return lax.dot_general(
        left, right, (((0,), (0,)), ((), ())), preferred_element_type=jnp.float32
    )


def shards(
    hidden,
    grad_out,
    query_weight,
    key_weight,
    value_weight,
    out_weight,
    neighbour_states,
    block_owner,
    slot_target,
):
    full_hidden, full_grad = side_by_side((hidden, grad_out), "tensor", 1, 0)
    out_gathered = lax.all_gather(out_weight, "dp", axis=1, tiled=True)
    dp_count = lax.axis_size("dp")
    my_index = lax.axis_index("dp")
    block_count, block_len, width_part = neighbour_states.shape
    block_ids = jnp.arange(block_count, dtype=jnp.int32)
    owner_gap = (block_owner[0] - my_index + dp_count) % dp_count
    target_gap = (my_index - slot_target[0] + dp_count) % dp_count
    pair_ids = jnp.arange(CAP, dtype=jnp.int32)
    flat_states = neighbour_states.reshape(block_count, block_len * width_part)
    delivered = jnp.zeros((block_count, block_len * width_part), jnp.float32)
    for offset in range(1, WINDOW + 1):
        send_table = (
            (target_gap[None, :] == offset) & ((block_ids % CAP)[None, :] == pair_ids[:, None])
        ).astype(jnp.bfloat16)
        receive_table = (
            (owner_gap[:, None] == offset) & ((block_ids % CAP)[:, None] == pair_ids[None, :])
        ).astype(jnp.bfloat16)
        outgoing = jnp.dot(send_table, flat_states, preferred_element_type=jnp.float32).astype(
            jnp.bfloat16
        )
        incoming = shifted(outgoing, "dp", -offset)
        delivered = delivered + jnp.dot(receive_table, incoming, preferred_element_type=jnp.float32)
    delivered = delivered.astype(jnp.bfloat16)
    neighbours = gathered_copies(
        delivered.reshape(block_count * block_len, width_part), "tensor", 1
    )
    query = jnp.dot(full_hidden, query_weight, preferred_element_type=jnp.float32).astype(
        jnp.bfloat16
    )
    key_rows = jnp.dot(neighbours, key_weight, preferred_element_type=jnp.float32).astype(
        jnp.bfloat16
    )
    value_rows = jnp.dot(neighbours, value_weight, preferred_element_type=jnp.float32).astype(
        jnp.bfloat16
    )
    local_heads = HEADS // lax.axis_size("tensor")
    head_size = query.shape[1] // local_heads
    span_count = query.shape[0] // SPAN
    score_scale = 1.0 / math.sqrt(head_size)
    query_heads = query.reshape(span_count, SPAN, local_heads, head_size)
    key_heads = key_rows.reshape(span_count, K_NB * block_len, local_heads, head_size)
    value_heads = value_rows.reshape(span_count, K_NB * block_len, local_heads, head_size)
    scores = (
        jnp.einsum("cqhd,ckhd->chqk", query_heads, key_heads, preferred_element_type=jnp.float32)
        * score_scale
    )
    highest = jnp.max(scores, axis=-1, keepdims=True)
    expanded = jnp.exp(scores - highest)
    probs = expanded / jnp.sum(expanded, axis=-1, keepdims=True)
    probs_low = probs.astype(jnp.bfloat16)
    attended = (
        jnp.einsum("chqk,ckhd->cqhd", probs_low, value_heads, preferred_element_type=jnp.float32)
        .astype(jnp.bfloat16)
        .reshape(query.shape)
    )
    out_partial = jnp.dot(attended, out_gathered, preferred_element_type=jnp.float32).astype(
        jnp.bfloat16
    )
    grad_attended = contract_last(full_grad, out_gathered).astype(jnp.bfloat16)
    grad_heads = grad_attended.reshape(query_heads.shape)
    grad_probs = jnp.einsum(
        "cqhd,ckhd->chqk", grad_heads, value_heads, preferred_element_type=jnp.float32
    )
    grad_scores = (
        probs * (grad_probs - jnp.sum(probs * grad_probs, axis=-1, keepdims=True)) * score_scale
    ).astype(jnp.bfloat16)
    grad_query = (
        jnp.einsum("chqk,ckhd->cqhd", grad_scores, key_heads, preferred_element_type=jnp.float32)
        .astype(jnp.bfloat16)
        .reshape(query.shape)
    )
    grad_key = (
        jnp.einsum("chqk,cqhd->ckhd", grad_scores, query_heads, preferred_element_type=jnp.float32)
        .astype(jnp.bfloat16)
        .reshape(key_rows.shape)
    )
    grad_value = (
        jnp.einsum("chqk,cqhd->ckhd", probs_low, grad_heads, preferred_element_type=jnp.float32)
        .astype(jnp.bfloat16)
        .reshape(value_rows.shape)
    )
    hidden_partial = contract_last(grad_query, query_weight).astype(jnp.bfloat16)
    states_partial = (
        contract_last(grad_key, key_weight) + contract_last(grad_value, value_weight)
    ).astype(jnp.bfloat16)
    out_summed, hidden_summed, states_summed = (
        *sent_together((out_partial, hidden_partial), "tensor", 1, 0),
        summed_on_arrival(states_partial, "tensor", 1),
    )
    cross_out = out_summed.astype(jnp.bfloat16)
    grad_hidden = hidden_summed.astype(jnp.bfloat16)
    grad_rows = states_summed.astype(jnp.bfloat16).reshape(block_count, block_len * width_part)
    grad_states = jnp.zeros((block_count, block_len * width_part), jnp.float32)
    for offset in range(1, WINDOW + 1):
        send_table = (
            (target_gap[None, :] == offset) & ((block_ids % CAP)[None, :] == pair_ids[:, None])
        ).astype(jnp.bfloat16)
        receive_table = (
            (owner_gap[:, None] == offset) & ((block_ids % CAP)[:, None] == pair_ids[None, :])
        ).astype(jnp.bfloat16)
        returning = contract_first(receive_table, grad_rows).astype(jnp.bfloat16)
        returned = shifted(returning, "dp", offset)
        grad_states = grad_states + contract_first(send_table, returned)
    grad_states = grad_states.astype(jnp.bfloat16)
    return (cross_out, grad_hidden, grad_states.reshape(block_count, block_len, width_part))


def solution(mesh):
    placed = (
        P("dp", "tensor"),
        P("dp", "tensor"),
        P(None, "tensor"),
        P(None, "tensor"),
        P(None, "tensor"),
        P("tensor", "dp"),
        P("dp", None, "tensor"),
        P("dp", None),
        P("dp", None),
    )
    return jax.shard_map(
        shards,
        mesh=mesh,
        in_specs=placed,
        out_specs=(P("dp", "tensor"), P("dp", "tensor"), P("dp", None, "tensor")),
        check_vma=False,
    )
```

profile of v0, /device:TPU:32, one launch (start us, length us, event | category | flops | bytes accessed | tf_op | source)
XLA Modules:
  0.0 235.4 jit_solution(10116544466631510508)
XLA Ops:
  7.2 2.0 pad_maximum_fusion.1
  9.3 0.7 all-gather.5.cloned.1.call-update
  10.0 1.1 copy.37
  11.7 1.8 collective-permute-start
  13.8 0.9 collective-permute-start.1
  14.9 0.4 collective-permute-start.2
  15.7 8.1 %collective-permute-start.3 = (bf16[2,24576]{1,0:T(2,128)(2,1)S(1)}, bf16[2,24576]{1,0:T(2,128)(2,1)S(1)}, u32[]{:S(2)}, u32[]{:S(2)}) collective-permute-start(bf16[2,24576]{1,0:T(2,128)(2,1)S(1)} %convolution_convert_fusion.4), channel_id=1, source_target_pairs={{0,240},{4,244},{8,248},{12,252},{16,0},{20,4},{24,8},{28,12},{32,... | collective-permute-start | bytes 294920 | tf_op jit(solution)/shard_map/ppermute | solution.py:25
  23.8 2.5 %collective-permute-done.3 = bf16[2,24576]{1,0:T(2,128)(2,1)S(1)} collective-permute-done((bf16[2,24576]{1,0:T(2,128)(2,1)S(1)}, bf16[2,24576]{1,0:T(2,128)(2,1)S(1)}, u32[]{:S(2)}, u32[]{:S(2)}) %collective-permute-start.3) | collective-permute-done | bytes 98336 | tf_op jit(solution)/shard_map/ppermute | solution.py:25
  27.3 0.4 fusion.6
  28.1 25.8 %all_to_all.15 = bf16[4,512,192]{1,2,0:T(8,128)(2,1)S(1)} all-to-all(bf16[4,512,192]{1,2,0:T(8,128)(2,1)S(1)} %broadcast_in_dim.2), channel_id=1, replica_groups=mesh['dp'=64,'tensor'=4] {'tensor'}, dimensions={0} | all-to-all | bytes 1572864 | tf_op jit(solution)/shard_map/all_to_all | solution.py:36
  53.9 1.0 fusion.10
  55.2 1.1 copy-done.6
  56.3 1.0 fusion.9
  57.3 1.3 copy.58
  58.6 5.0 %fusion.18 = bf16[16,8,8,128]{3,1,2,0:T(8,128)(2,1)S(1)} fusion(bf16[4096,1024]{1,0:T(8,128)(2,1)} %param.11, bf16[256,4096]{1,0:T(8,128)(2,1)} %all-gather.3.cloned.1.call-done), kind=kOutput, calls=%fused_computation.42 | convolution fusion | flops 1073872896 | bytes 9699328 | tf_op jit(solution)/shard_map/dot_general | solution.py:114
  63.6 0.5 convolution_multiply_fusion
  64.1 1.0 copy-done.2
  65.1 1.2 fusion.115
  66.3 3.8 %fusion.20 = bf16[2,64,8,128]{3,1,2,0:T(8,128)(2,1)S(1)} fusion(bf16[2,256,8,128]{3,2,1,0:T(8,128)(2,1)} %bitcast.101, f32[2,8,64]{2,1,0:T(8,128)S(1)} %get-tuple-element.24, f32[2,8,64,256]{3,2,1,0:T(8,128)} %copy-done.2), kind=kOutput, calls=%fused_computation.44 | convolution fusion | flops 68027648 | bytes 2363392 | tf_op jit(solution)/shard_map/chqk,ckhd->cqhd/dot_general | solution.py:139
  70.3 69.9 %all-gather.5.cloned.1.call-done = bf16[1024,4096]{0,1:T(8,128)(2,1)} async-done(((bf16[1024,64]{0,1:T(8,128)(2,1)}), bf16[1024,4096]{0,1:T(8,128)(2,1)}) %all-gather.5.cloned.1.call-update) | async-done | bytes 8388624 | tf_op jit(solution)/shard_map/all_gather | solution.py:88
  140.2 5.0 %fusion.19 = bf16[16,8,8,128]{3,1,2,0:T(8,128)(2,1)S(1)} fusion(bf16[1024,4096]{0,1:T(8,128)(2,1)} %all-gather.5.cloned.1.call-done, bf16[256,4096]{1,0:T(8,128)(2,1)} %all-gather.3.cloned.1.call-done), kind=kOutput, calls=%fused_computation.43 | convolution fusion | flops 1073872896 | bytes 9699328 | tf_op jit(solution)/shard_map/dot_general | solution.py:65
  145.3 1.4 fusion.33
  146.7 4.7 %fusion.12 = bf16[2,256,8,128]{1,3,2,0:T(8,128)(2,1)} fusion(bf16[2,64,8,128]{3,2,1,0:T(8,128)(2,1)S(1)} %bitcast.108, f32[2,8,64]{2,1,0:T(8,128)S(1)} %get-tuple-element.24, f32[2,8,64,256]{3,2,1,0:T(8,128)} %copy-done.2), kind=kOutput, calls=%fused_computation.31 | convolution fusion | flops 68420864 | bytes 2363392 | tf_op jit(solution)/shard_map/chqk,cqhd->ckhd/dot_general | solution.py:165
  151.4 7.6 %fusion.21 = bf16[2,64,8,128]{3,1,2,0:T(8,128)(2,1)S(1)} fusion(f32[2,8,64,256]{3,2,1,0:T(8,128)} %fusion.33, bf16[2,256,8,128]{3,2,1,0:T(8,128)(2,1)S(1)} %bitcast.100, f32[2,8,64,256]{3,2,1,0:T(8,128)} %get-tuple-element.25, f32[2,8,64]{2,1,0:T(8,128)S(1)} %get-tuple-element.24), kind=kOutput, calls=%fused_computation.45 | convolution fusion | flops 69076224 | bytes 3411968 | tf_op jit(solution)/shard_map/chqk,ckhd->cqhd/dot_general | solution.py:155
  159.0 7.9 %fusion.11 = bf16[2,256,8,128]{1,3,2,0:T(8,128)(2,1)S(1)} fusion(f32[2,8,64,256]{3,2,1,0:T(8,128)} %fusion.33, bf16[2,64,8,128]{3,2,1,0:T(8,128)(2,1)S(1)} %bitcast.105, f32[2,8,64,256]{3,2,1,0:T(8,128)} %get-tuple-element.25, f32[2,8,64]{2,1,0:T(8,128)S(1)} %get-tuple-element.24), kind=kOutput, calls=%fused_computation.30 | convolution fusion | flops 69469440 | bytes 3411968 | tf_op jit(solution)/shard_map/chqk,cqhd->ckhd/dot_general | solution.py:160
  166.9 1.5 copy.49
  168.6 2.4 %copy.51 = bf16[2,256,8,128]{3,2,1,0:T(8,128)(2,1)} copy(bf16[2,256,8,128]{1,3,2,0:T(8,128)(2,1)} %fusion.12) | data formatting | bytes 2097152 | tf_op jit(solution)/shard_map/convert_element_type | solution.py:166
  171.0 2.4 %fusion.24 = f32[512,768]{1,0:T(8,128)S(1)} fusion(bf16[768,1024]{1,0:T(8,128)(2,1)S(1)} %copy-done, bf16[64,8,8,128]{3,2,1,0:T(8,128)(2,1)} %bitcast.109), kind=kOutput, calls=%fused_computation.48 | convolution fusion | flops 805306368 | bytes 4194304 | tf_op jit(solution)/shard_map/dot_general | solution.py:65
  173.4 1.0 add_convert_fusion
  174.4 1.2 copy.52
  175.7 4.4 %all-to-all-start.2 = ((bf16[4,512,192]{1,2,0:T(8,128)(2,1)}), bf16[4,512,192]{1,2,0:T(8,128)(2,1)S(1)}, u32[]{:S(2)}, u32[]{:S(2)}) async-start(bf16[4,512,192]{1,2,0:T(8,128)(2,1)} %bitcast.14), calls=%async_computation.2 | async-start | bytes 1572864 | tf_op jit(solution)/shard_map/all_to_all | solution.py:51
  180.1 6.3 %convolution_convert_fusion.8 = bf16[128,4096]{1,0:T(8,128)(2,1)S(1)} fusion(bf16[4096,1024]{1,0:T(8,128)(2,1)} %param.11, bf16[16,8,8,128]{3,2,1,0:T(8,128)(2,1)S(1)} %bitcast.106), kind=kOutput, calls=%fused_computation.18 | convolution fusion | flops 1074266112 | bytes 9699328 | tf_op jit(solution)/shard_map/dot_general | solution.py:65
  186.3 6.3 %convolution_convert_fusion.9 = bf16[128,4096]{1,0:T(8,128)(2,1)S(1)} fusion(bf16[1024,4096]{0,1:T(8,128)(2,1)} %all-gather.5.cloned.1.call-done, bf16[16,8,8,128]{3,2,1,0:T(8,128)(2,1)S(1)} %bitcast.103), kind=kOutput, calls=%fused_computation.19 | convolution fusion | flops 1074266112 | bytes 9699328 | tf_op jit(solution)/shard_map/dot_general | solution.py:143
  192.8 1.5 copy.97
  194.4 4.8 %all-to-all-start.1 = ((bf16[4,256,1024]{2,1,0:T(8,128)(2,1)}), bf16[4,256,1024]{2,1,0:T(8,128)(2,1)}, u32[]{:S(2)}, u32[]{:S(2)}) async-start(bf16[4,256,1024]{2,1,0:T(8,128)(2,1)} %bitcast.97), calls=%async_computation.1 | async-start | bytes 4194304 | tf_op jit(solution)/shard_map/all_to_all | solution.py:51
  199.8 0.4 convolution_convert_fusion
  200.2 1.5 collective-permute-start.7
  201.7 0.4 convolution_convert_fusion.1
  202.1 0.4 convolution_convert_fusion.2
  202.4 0.4 convolution_convert_fusion.3
  203.1 1.7 collective-permute-start.6
  204.9 2.5 %collective-permute-done.7 = bf16[2,24576]{1,0:T(2,128)(2,1)S(1)} collective-permute-done((bf16[2,24576]{1,0:T(2,128)(2,1)S(1)}, bf16[2,24576]{1,0:T(2,128)(2,1)S(1)}, u32[]{:S(2)}, u32[]{:S(2)}) %collective-permute-start.7) | collective-permute-done | bytes 98336 | tf_op jit(solution)/shard_map/ppermute | solution.py:25
  207.7 3.7 %collective-permute-done.6 = bf16[2,24576]{1,0:T(2,128)(2,1)S(1)} collective-permute-done((bf16[2,24576]{1,0:T(2,128)(2,1)S(1)}, bf16[2,24576]{1,0:T(2,128)(2,1)S(1)}, u32[]{:S(2)}, u32[]{:S(2)}) %collective-permute-start.6) | collective-permute-done | bytes 98336 | tf_op jit(solution)/shard_map/ppermute | solution.py:25
  212.1 0.3 fusion.7
  212.7 0.8 copy.54
  213.6 12.1 %all-to-all-done.1 = bf16[4,256,1024]{2,1,0:T(8,128)(2,1)} async-done(((bf16[4,256,1024]{2,1,0:T(8,128)(2,1)}), bf16[4,256,1024]{2,1,0:T(8,128)(2,1)}, u32[]{:S(2)}, u32[]{:S(2)}) %all-to-all-start.1) | async-done | bytes 2097184 | tf_op jit(solution)/shard_map/all_to_all | solution.py:51
  225.7 2.0 reduce.1
  227.7 0.8 fusion.114
  (55 shorter events, 6.0 us)
Async XLA Ops:
  7.2 46.7 %copy-start = (bf16[768,1024]{1,0:T(8,128)(2,1)S(1)}, bf16[768,1024]{1,0:T(8,128)(2,1)}, u32[]{:S(2)}) copy-start(bf16[768,1024]{1,0:T(8,128)(2,1)} %param.12) | copy-start | bytes 4718596
  7.2 4.2 %copy-start.4 = (s32[1,4]{1,0:T(1,128)S(1)}, s32[1,4]{1,0:T(1,128)}, u32[]{:S(2)}) copy-start(s32[1,4]{1,0:T(1,128)} %param.17) | copy-start | bytes 52
  7.2 16.6 %copy-start.5 = (s32[1,4]{1,0:T(1,128)S(1)}, s32[1,4]{1,0:T(1,128)}, u32[]{:S(2)}) copy-start(s32[1,4]{1,0:T(1,128)} %param.16) | copy-start | bytes 52
  7.2 51.4 %all-gather.3.cloned.1.call-start = ((), (), s32[]{:S(2)}) async-start(), calls=%async_computation.3 | async-start | bytes 2621440 | tf_op jit(solution)/shard_map/all_gather | solution.py:16
  9.3 130.9 %all-gather.5.cloned.1.call-start = ((), (), s32[]{:S(2)}) async-start(), calls=%async_computation.4 | async-start | bytes 8519680 | tf_op jit(solution)/shard_map/all_gather | solution.py:88
  11.7 15.6 %collective-permute-start = (bf16[2,24576]{1,0:T(2,128)(2,1)S(1)}, bf16[2,24576]{1,0:T(2,128)(2,1)S(1)}, u32[]{:S(2)}, u32[]{:S(2)}) collective-permute-start(bf16[2,24576]{1,0:T(2,128)(2,1)S(1)} %convolution_convert_fusion.7), channel_id=1, source_target_pairs={{0,252},{4,0},{8,4},{12,8},{16,12},{20,16},{24,20},{28,24},{32,28}... | collective-permute-start | bytes 294920 | tf_op jit(solution)/shard_map/ppermute | solution.py:25
  13.8 13.1 %collective-permute-start.1 = (bf16[2,24576]{1,0:T(2,128)(2,1)S(1)}, bf16[2,24576]{1,0:T(2,128)(2,1)S(1)}, u32[]{:S(2)}, u32[]{:S(2)}) collective-permute-start(bf16[2,24576]{1,0:T(2,128)(2,1)S(1)} %convolution_convert_fusion.6), channel_id=1, source_target_pairs={{0,248},{4,252},{8,0},{12,4},{16,8},{20,12},{24,16},{28,20},{32,24... | collective-permute-start | bytes 294920 | tf_op jit(solution)/shard_map/ppermute | solution.py:25
  14.9 11.6 %collective-permute-start.2 = (bf16[2,24576]{1,0:T(2,128)(2,1)S(1)}, bf16[2,24576]{1,0:T(2,128)(2,1)S(1)}, u32[]{:S(2)}, u32[]{:S(2)}) collective-permute-start(bf16[2,24576]{1,0:T(2,128)(2,1)S(1)} %convolution_convert_fusion.5), channel_id=1, source_target_pairs={{0,244},{4,248},{8,252},{12,0},{16,4},{20,8},{24,12},{28,16},{32,2... | collective-permute-start | bytes 294920 | tf_op jit(solution)/shard_map/ppermute | solution.py:25
  15.7 10.6 %collective-permute-start.3 = (bf16[2,24576]{1,0:T(2,128)(2,1)S(1)}, bf16[2,24576]{1,0:T(2,128)(2,1)S(1)}, u32[]{:S(2)}, u32[]{:S(2)}) collective-permute-start(bf16[2,24576]{1,0:T(2,128)(2,1)S(1)} %convolution_convert_fusion.4), channel_id=1, source_target_pairs={{0,240},{4,244},{8,248},{12,252},{16,0},{20,4},{24,8},{28,12},{32,... | collective-permute-start | bytes 294920 | tf_op jit(solution)/shard_map/ppermute | solution.py:25
  54.9 1.4 copy-start.6
  64.1 1.0 copy-start.2
  140.2 5.1 %copy-start.1 = (bf16[64,8,8,128]{3,2,1,0:T(8,128)(2,1)S(1)}, bf16[64,8,8,128]{3,2,1,0:T(8,128)(2,1)}, u32[]{:S(2)}) copy-start(bf16[64,8,8,128]{3,2,1,0:T(8,128)(2,1)} %copy.58) | copy-start | bytes 3145732
  171.0 2.4 %copy-start.3 = (bf16[2,256,8,128]{3,2,1,0:T(8,128)(2,1)S(1)}, bf16[2,256,8,128]{3,2,1,0:T(8,128)(2,1)}, u32[]{:S(2)}) copy-start(bf16[2,256,8,128]{3,2,1,0:T(8,128)(2,1)} %copy.51) | copy-start | bytes 3145732
  171.0 2.4 %copy-start.7 = (bf16[768,1024]{1,0:T(8,128)(2,1)S(1)}, bf16[768,1024]{1,0:T(8,128)(2,1)}, u32[]{:S(2)}) copy-start(bf16[768,1024]{1,0:T(8,128)(2,1)} %param.13) | copy-start | bytes 4718596
  175.7 18.7 %all-to-all-start.2 = ((bf16[4,512,192]{1,2,0:T(8,128)(2,1)}), bf16[4,512,192]{1,2,0:T(8,128)(2,1)S(1)}, u32[]{:S(2)}, u32[]{:S(2)}) async-start(bf16[4,512,192]{1,2,0:T(8,128)(2,1)} %bitcast.14), calls=%async_computation.2 | async-start | bytes 1572864 | tf_op jit(solution)/shard_map/all_to_all | solution.py:51
  194.4 31.3 %all-to-all-start.1 = ((bf16[4,256,1024]{2,1,0:T(8,128)(2,1)}), bf16[4,256,1024]{2,1,0:T(8,128)(2,1)}, u32[]{:S(2)}, u32[]{:S(2)}) async-start(bf16[4,256,1024]{2,1,0:T(8,128)(2,1)} %bitcast.97), calls=%async_computation.1 | async-start | bytes 4194304 | tf_op jit(solution)/shard_map/all_to_all | solution.py:51
  200.2 7.2 %collective-permute-start.7 = (bf16[2,24576]{1,0:T(2,128)(2,1)S(1)}, bf16[2,24576]{1,0:T(2,128)(2,1)S(1)}, u32[]{:S(2)}, u32[]{:S(2)}) collective-permute-start(bf16[2,24576]{1,0:T(2,128)(2,1)S(1)} %convolution_convert_fusion), channel_id=1, source_target_pairs={{0,16},{4,20},{8,24},{12,28},{16,32},{20,36},{24,40},{28,44},{32,4... | collective-permute-start | bytes 294920 | tf_op jit(solution)/shard_map/ppermute | solution.py:25
  202.8 9.3 %collective-permute-start.4 = (bf16[2,24576]{1,0:T(2,128)(2,1)S(1)}, bf16[2,24576]{1,0:T(2,128)(2,1)S(1)}, u32[]{:S(2)}, u32[]{:S(2)}) collective-permute-start(bf16[2,24576]{1,0:T(2,128)(2,1)S(1)} %convolution_convert_fusion.3), channel_id=1, source_target_pairs={{0,4},{4,8},{8,12},{12,16},{16,20},{20,24},{24,28},{28,32},{32,36}... | collective-permute-start | bytes 294920 | tf_op jit(solution)/shard_map/ppermute | solution.py:25
  202.9 8.9 %collective-permute-start.5 = (bf16[2,24576]{1,0:T(2,128)(2,1)S(1)}, bf16[2,24576]{1,0:T(2,128)(2,1)S(1)}, u32[]{:S(2)}, u32[]{:S(2)}) collective-permute-start(bf16[2,24576]{1,0:T(2,128)(2,1)S(1)} %convolution_convert_fusion.2), channel_id=1, source_target_pairs={{0,8},{4,12},{8,16},{12,20},{16,24},{20,28},{24,32},{28,36},{32,40... | collective-permute-start | bytes 294920 | tf_op jit(solution)/shard_map/ppermute | solution.py:25
  203.1 8.2 %collective-permute-start.6 = (bf16[2,24576]{1,0:T(2,128)(2,1)S(1)}, bf16[2,24576]{1,0:T(2,128)(2,1)S(1)}, u32[]{:S(2)}, u32[]{:S(2)}) collective-permute-start(bf16[2,24576]{1,0:T(2,128)(2,1)S(1)} %convolution_convert_fusion.1), channel_id=1, source_target_pairs={{0,12},{4,16},{8,20},{12,24},{16,28},{20,32},{24,36},{28,40},{32,4... | collective-permute-start | bytes 294920 | tf_op jit(solution)/shard_map/ppermute | solution.py:25
Sparse Core Ops, SparseCore 0:
  9.8 44.4 all-gather.2
  57.1 83.0 all-gather.4
where the time goes:
time: 236 us; the launch traced here: 235 us
  waiting for transfers between devices  91.5 us (39%)
  matrix products  59 us (25%)
  blocking collectives  25.8 us (11%)
  starting transfers between devices  24.1 us (10%)
  local copies, waits for them, and re-layouts  15 us (6%)
  between operations  14.5 us (6%)
  other arithmetic  5.61 us (2%)
    all_gather x1, waiting for transfers between devices, shards(): out_gathered = lax.all_gather(out_weight, 'dp', axis=1, tiled=True)  69.9 us
    all_to_all x1, blocking collectives, from_everyone(): return lax.all_to_all(copies, axis, split_axis=0, concat_axis=0, tiled=True)  25.8 us
    ppermute x8, starting transfers between devices, shifted(): lax.ppermute(x, axis, [(i, (i + by) % devices) for i in range(devices)])  14.8 us
    dot_general x4, matrix products, contract_last(): lax.dot_general(left, right, (((1,), (1,)), ((), ())), preferred_element_...  14.7 us
    all_to_all x2, waiting for transfers between devices, summed_on_arrival(): lax.all_to_all(tiles, axis, split_axis=0, concat_axis=0, tiled=True)  12.1 us
    all_to_all x2, starting transfers between devices, summed_on_arrival(): lax.all_to_all(tiles, axis, split_axis=0, concat_axis=0, tiled=True)  9.18 us
    ppermute x8, waiting for transfers between devices, shifted(): lax.ppermute(x, axis, [(i, (i + by) % devices) for i in range(devices)])  8.77 us
    dot_general x1, matrix products, shards(): jnp.einsum('chqk,cqhd->ckhd', grad_scores, query_heads, preferred_element...  7.92 us
  transfers between devices with their start and end apart: 12, of which 6 were waited for; matrix products, arithmetic and copies ran while one was open for 16% of the time, Pallas kernels for 0%

commit v1 on v0

--- a/solution.py
+++ b/solution.py
@@ -85,7 +85,9 @@
     slot_target,
 ):
     full_hidden, full_grad = side_by_side((hidden, grad_out), "tensor", 1, 0)
-    out_gathered = lax.all_gather(out_weight, "dp", axis=1, tiled=True)
+    out_gathered = jnp.concatenate(
+        lax.all_to_all(jnp.stack([out_weight] * lax.axis_size("dp")), "dp", 0, 0), axis=1
+    )
     dp_count = lax.axis_size("dp")
     my_index = lax.axis_index("dp")
     block_count, block_len, width_part = neighbour_states.shape

time: 236 us -> 341 us (1.44)
  waiting for transfers between devices: 91.5 us -> 186 us
  starting transfers between devices: 24.1 us -> 37 us
  blocking collectives: 25.8 us -> 14.6 us
  matrix products: 59 us -> 64.7 us
    all_to_all x0 -> x1, waiting for transfers between devices: none -> 139 us  [shards(): lax.all_to_all(jnp.stack([out_weight] * lax.axis_size('dp')), 'dp', 0, 0)]
    all_gather x1 -> x0, waiting for transfers between devices: 69.9 us -> none  [shards(): out_gathered = lax.all_gather(out_weight, 'dp', axis=1, tiled=True)]
    all_gather x1, waiting for transfers between devices: 0.01 us -> 29.3 us  [side_by_side(): lax.all_gather(both, axis, axis=dim, tiled=True)]
    all_to_all x1, blocking collectives: 25.8 us -> 14.6 us  [from_everyone(): return lax.all_to_all(copies, axis, split_axis=0, concat_axis=0, tiled=True)]
    all_to_all x0 -> x1, starting transfers between devices: none -> 10.8 us  [shards(): lax.all_to_all(jnp.stack([out_weight] * lax.axis_size('dp')), 'dp', 0, 0)]
    another operation x0 -> x1, local copies, waits for them, and re-layouts: none -> 4.29 us  [shards(): jnp.stack([out_weight] * lax.axis_size('dp'))]
  transfers between devices with their start and end apart: 12 -> 12, of which waited for: 6 -> 8; matrix products, arithmetic and copies ran while one was open for 16% -> 11% of each run, Pallas kernels for 0% -> 0%
where the time goes in v1:
time: 341 us; the launch traced here: 340 us
  waiting for transfers between devices  186 us (55%)
  matrix products  64.7 us (19%)
  starting transfers between devices  37 us (11%)
  local copies, waits for them, and re-layouts  18.4 us (5%)
  blocking collectives  14.6 us (4%)
  between operations  14.5 us (4%)
  other arithmetic  5.23 us (2%)
    all_to_all x1, waiting for transfers between devices, shards(): lax.all_to_all(jnp.stack([out_weight] * lax.axis_size('dp')), 'dp', 0, 0)  139 us
    all_gather x1, waiting for transfers between devices, side_by_side(): lax.all_gather(both, axis, axis=dim, tiled=True)  29.3 us
    dot_general x4, matrix products, contract_last(): lax.dot_general(left, right, (((1,), (1,)), ((), ())), preferred_element_...  18.1 us
    ppermute x8, starting transfers between devices, shifted(): lax.ppermute(x, axis, [(i, (i + by) % devices) for i in range(devices)])  17.7 us
    all_to_all x1, blocking collectives, from_everyone(): return lax.all_to_all(copies, axis, split_axis=0, concat_axis=0, tiled=True)  14.6 us
    all_to_all x1, starting transfers between devices, shards(): lax.all_to_all(jnp.stack([out_weight] * lax.axis_size('dp')), 'dp', 0, 0)  10.8 us
    all_to_all x2, waiting for transfers between devices, summed_on_arrival(): lax.all_to_all(tiles, axis, split_axis=0, concat_axis=0, tiled=True)  10.6 us
    dot_general x1, matrix products, shards(): jnp.einsum('chqk,cqhd->ckhd', grad_scores, query_heads, preferred_element...  8.95 us
  transfers between devices with their start and end apart: 12, of which 8 were waited for; matrix products, arithmetic and copies ran while one was open for 11% of the time, Pallas kernels for 0%

profile of v1, /device:TPU:32, one launch (start us, length us, event | category | flops | bytes accessed | tf_op | source)
XLA Modules:
  0.0 340.3 jit_solution(2943615281487932775)
XLA Ops:
  7.2 0.8 compare_bitcast_fusion.3
  8.0 1.1 copy.38
  9.6 2.4 collective-permute-start.1
  12.6 8.0 %collective-permute-start.3 = (bf16[2,24576]{1,0:T(2,128)(2,1)S(1)}, bf16[2,24576]{1,0:T(2,128)(2,1)S(1)}, u32[]{:S(2)}, u32[]{:S(2)}) collective-permute-start(bf16[2,24576]{1,0:T(2,128)(2,1)S(1)} %convolution_convert_fusion.4), channel_id=1, source_target_pairs={{0,240},{4,244},{8,248},{12,252},{16,0},{20,4},{24,8},{28,12},{32,... | collective-permute-start | bytes 294920 | tf_op jit(solution)/shard_map/ppermute | solution.py:25
  20.9 1.5 collective-permute-start
  23.5 1.2 collective-permute-done
  25.5 14.6 %all_to_all.20 = bf16[4,512,192]{1,2,0:T(8,128)(2,1)S(1)} all-to-all(bf16[4,512,192]{1,2,0:T(8,128)(2,1)S(1)} %broadcast_in_dim.2), channel_id=1, replica_groups=mesh['dp'=64,'tensor'=4] {'tensor'}, dimensions={0} | all-to-all | bytes 1572864 | tf_op jit(solution)/shard_map/all_to_all | solution.py:36
  40.1 4.3 %stack.2 = bf16[64,1024,64]{1,2,0:T(8,128)(2,1)} broadcast(bf16[1024,64]{0,1:T(8,128)(2,1)S(1)} %copy-done.6), dimensions={1,2} | broadcast | bytes 8519680 | tf_op jit(solution)/shard_map/stack | solution.py:89
  44.4 10.8 %all-to-all-start.1 = ((bf16[64,1024,64]{1,2,0:T(8,128)(2,1)}), bf16[64,1024,64]{1,2,0:T(8,128)(2,1)}, u32[]{:S(2)}, u32[]{:S(2)}) async-start(bf16[64,1024,64]{1,2,0:T(8,128)(2,1)} %stack.2), calls=%async_computation.1 | async-start | bytes 16777216 | tf_op jit(solution)/shard_map/all_to_all | solution.py:89
  55.5 0.8 pad_maximum_fusion.1
  56.3 2.4 fusion.9
  58.8 1.2 copy.59
  60.0 1.0 fusion.10
  61.3 29.3 %all-gather.2.cloned.1.call-done = bf16[256,4096]{1,0:T(8,128)(2,1)} async-done(((bf16[256,1024]{1,0:T(8,128)(2,1)}), bf16[256,4096]{1,0:T(8,128)(2,1)}) %all-gather.2.cloned.1.call-update) | async-done | bytes 2097168 | tf_op jit(solution)/shard_map/all_gather | solution.py:16
  90.6 5.0 %fusion.18 = bf16[16,8,8,128]{3,1,2,0:T(8,128)(2,1)S(1)} fusion(bf16[4096,1024]{1,0:T(8,128)(2,1)} %param.11, bf16[256,4096]{1,0:T(8,128)(2,1)} %all-gather.2.cloned.1.call-done), kind=kOutput, calls=%fused_computation.42 | convolution fusion | flops 1073872896 | bytes 9699328 | tf_op jit(solution)/shard_map/dot_general | solution.py:116
  95.7 0.5 convolution_multiply_fusion
  96.2 1.0 copy-done.2
  97.1 1.2 fusion.115
  98.3 3.7 %fusion.20 = bf16[2,64,8,128]{3,1,2,0:T(8,128)(2,1)S(1)} fusion(bf16[2,256,8,128]{3,2,1,0:T(8,128)(2,1)} %bitcast.104, f32[2,8,64]{2,1,0:T(8,128)S(1)} %get-tuple-element.24, f32[2,8,64,256]{3,2,1,0:T(8,128)} %copy-done.2), kind=kOutput, calls=%fused_computation.44 | convolution fusion | flops 68027648 | bytes 2363392 | tf_op jit(solution)/shard_map/chqk,ckhd->cqhd/dot_general | solution.py:141
  102.2 139.3 %all-to-all-done.1 = bf16[64,1024,64]{1,2,0:T(8,128)(2,1)} async-done(((bf16[64,1024,64]{1,2,0:T(8,128)(2,1)}), bf16[64,1024,64]{1,2,0:T(8,128)(2,1)}, u32[]{:S(2)}, u32[]{:S(2)}) %all-to-all-start.1) | async-done | bytes 8388640 | tf_op jit(solution)/shard_map/all_to_all | solution.py:89
  241.5 5.0 %fusion.19 = bf16[16,8,8,128]{3,1,2,0:T(8,128)(2,1)S(1)} fusion(bf16[1024,4096]{0,1:T(8,128)(2,1)} %bitcast.10, bf16[256,4096]{1,0:T(8,128)(2,1)} %all-gather.2.cloned.1.call-done), kind=kOutput, calls=%fused_computation.43 | convolution fusion | flops 1073872896 | bytes 9699328 | tf_op jit(solution)/shard_map/dot_general | solution.py:65
  246.7 1.5 fusion.33
  248.2 4.6 %fusion.12 = bf16[2,256,8,128]{1,3,2,0:T(8,128)(2,1)} fusion(bf16[2,64,8,128]{3,2,1,0:T(8,128)(2,1)S(1)} %bitcast.110, f32[2,8,64]{2,1,0:T(8,128)S(1)} %get-tuple-element.24, f32[2,8,64,256]{3,2,1,0:T(8,128)} %copy-done.2), kind=kOutput, calls=%fused_computation.31 | convolution fusion | flops 68420864 | bytes 2363392 | tf_op jit(solution)/shard_map/chqk,cqhd->ckhd/dot_general | solution.py:167
  252.8 9.0 %fusion.11 = bf16[2,256,8,128]{1,3,2,0:T(8,128)(2,1)} fusion(f32[2,8,64,256]{3,2,1,0:T(8,128)} %fusion.33, bf16[2,64,8,128]{3,2,1,0:T(8,128)(2,1)S(1)} %bitcast.108, f32[2,8,64,256]{3,2,1,0:T(8,128)} %get-tuple-element.25, f32[2,8,64]{2,1,0:T(8,128)S(1)} %get-tuple-element.24), kind=kOutput, calls=%fused_computation.30 | convolution fusion | flops 69469440 | bytes 3411968 | tf_op jit(solution)/shard_map/chqk,cqhd->ckhd/dot_general | solution.py:162
  261.7 7.7 %fusion.21 = bf16[2,64,8,128]{3,1,2,0:T(8,128)(2,1)S(1)} fusion(f32[2,8,64,256]{3,2,1,0:T(8,128)} %fusion.33, bf16[2,256,8,128]{3,2,1,0:T(8,128)(2,1)S(1)} %bitcast.103, f32[2,8,64,256]{3,2,1,0:T(8,128)} %get-tuple-element.25, f32[2,8,64]{2,1,0:T(8,128)S(1)} %get-tuple-element.24), kind=kOutput, calls=%fused_computation.45 | convolution fusion | flops 69076224 | bytes 3411968 | tf_op jit(solution)/shard_map/chqk,ckhd->cqhd/dot_general | solution.py:157
  269.4 2.7 copy.50
  272.1 3.5 %fusion.24 = f32[512,768]{1,0:T(8,128)} fusion(bf16[768,1024]{1,0:T(8,128)(2,1)S(1)} %copy-done, bf16[64,8,8,128]{3,2,1,0:T(8,128)(2,1)} %bitcast.113), kind=kOutput, calls=%fused_computation.48 | convolution fusion | flops 805306368 | bytes 4194304 | tf_op jit(solution)/shard_map/dot_general | solution.py:65
  275.7 1.5 copy.52
  277.1 3.2 add_convert_fusion
  280.4 1.2 copy.53
  281.6 3.5 %all-to-all-start.3 = ((bf16[4,512,192]{1,2,0:T(8,128)(2,1)}), bf16[4,512,192]{1,2,0:T(8,128)(2,1)S(1)}, u32[]{:S(2)}, u32[]{:S(2)}) async-start(bf16[4,512,192]{1,2,0:T(8,128)(2,1)} %bitcast.17), calls=%async_computation.3 | async-start | bytes 1572864 | tf_op jit(solution)/shard_map/all_to_all | solution.py:51
  285.1 6.3 %convolution_convert_fusion.9 = bf16[128,4096]{1,0:T(8,128)(2,1)S(1)} fusion(bf16[1024,4096]{0,1:T(8,128)(2,1)} %bitcast.10, bf16[16,8,8,128]{3,2,1,0:T(8,128)(2,1)S(1)} %bitcast.106), kind=kOutput, calls=%fused_computation.19 | convolution fusion | flops 1074266112 | bytes 9699328 | tf_op jit(solution)/shard_map/dot_general | solution.py:145
  291.5 6.3 %convolution_convert_fusion.8 = bf16[128,4096]{1,0:T(8,128)(2,1)S(1)} fusion(bf16[4096,1024]{1,0:T(8,128)(2,1)} %param.11, bf16[16,8,8,128]{3,2,1,0:T(8,128)(2,1)S(1)} %bitcast.111), kind=kOutput, calls=%fused_computation.18 | convolution fusion | flops 1074266112 | bytes 9699328 | tf_op jit(solution)/shard_map/dot_general | solution.py:65
  298.0 1.6 copy.98
  299.6 4.8 %all-to-all-start.2 = ((bf16[4,256,1024]{2,1,0:T(8,128)(2,1)}), bf16[4,256,1024]{2,1,0:T(8,128)(2,1)}, u32[]{:S(2)}, u32[]{:S(2)}) async-start(bf16[4,256,1024]{2,1,0:T(8,128)(2,1)} %bitcast.100), calls=%async_computation.2 | async-start | bytes 4194304 | tf_op jit(solution)/shard_map/all_to_all | solution.py:51
  304.9 0.4 convolution_convert_fusion.1
  305.3 1.0 collective-permute-start.6
  306.7 0.4 convolution_convert_fusion
  307.4 1.3 collective-permute-start.5
  308.7 1.3 collective-permute-start.7
  310.0 2.1 collective-permute-start.4
  312.5 1.7 collective-permute-done.5
  314.6 3.0 collective-permute-done.7
  317.9 0.7 collective-permute-done.4
  319.2 0.8 copy.55
  320.0 10.6 %all-to-all-done.2 = bf16[4,256,1024]{2,1,0:T(8,128)(2,1)} async-done(((bf16[4,256,1024]{2,1,0:T(8,128)(2,1)}), bf16[4,256,1024]{2,1,0:T(8,128)(2,1)}, u32[]{:S(2)}, u32[]{:S(2)}) %all-to-all-start.2) | async-done | bytes 2097184 | tf_op jit(solution)/shard_map/all_to_all | solution.py:51
  330.6 2.0 reduce.1
  332.6 0.8 fusion.114
  (55 shorter events, 7.3 us)
Async XLA Ops:
  7.2 52.8 %copy-start = (bf16[768,1024]{1,0:T(8,128)(2,1)S(1)}, bf16[768,1024]{1,0:T(8,128)(2,1)}, u32[]{:S(2)}) copy-start(bf16[768,1024]{1,0:T(8,128)(2,1)} %param.12) | copy-start | bytes 4718596
  7.2 15.3 %copy-start.7 = (s32[1,4]{1,0:T(1,128)S(1)}, s32[1,4]{1,0:T(1,128)}, u32[]{:S(2)}) copy-start(s32[1,4]{1,0:T(1,128)} %param.16) | copy-start | bytes 52
  9.6 12.9 %collective-permute-start.1 = (bf16[2,24576]{1,0:T(2,128)(2,1)S(1)}, bf16[2,24576]{1,0:T(2,128)(2,1)S(1)}, u32[]{:S(2)}, u32[]{:S(2)}) collective-permute-start(bf16[2,24576]{1,0:T(2,128)(2,1)S(1)} %convolution_convert_fusion.6), channel_id=1, source_target_pairs={{0,248},{4,252},{8,0},{12,4},{16,8},{20,12},{24,16},{28,20},{32,24... | collective-permute-start | bytes 294920 | tf_op jit(solution)/shard_map/ppermute | solution.py:25
  12.3 10.5 %collective-permute-start.2 = (bf16[2,24576]{1,0:T(2,128)(2,1)S(1)}, bf16[2,24576]{1,0:T(2,128)(2,1)S(1)}, u32[]{:S(2)}, u32[]{:S(2)}) collective-permute-start(bf16[2,24576]{1,0:T(2,128)(2,1)S(1)} %convolution_convert_fusion.5), channel_id=1, source_target_pairs={{0,244},{4,248},{8,252},{12,0},{16,4},{20,8},{24,12},{28,16},{32,2... | collective-permute-start | bytes 294920 | tf_op jit(solution)/shard_map/ppermute | solution.py:25
  12.6 10.5 %collective-permute-start.3 = (bf16[2,24576]{1,0:T(2,128)(2,1)S(1)}, bf16[2,24576]{1,0:T(2,128)(2,1)S(1)}, u32[]{:S(2)}, u32[]{:S(2)}) collective-permute-start(bf16[2,24576]{1,0:T(2,128)(2,1)S(1)} %convolution_convert_fusion.4), channel_id=1, source_target_pairs={{0,240},{4,244},{8,248},{12,252},{16,0},{20,4},{24,8},{28,12},{32,... | collective-permute-start | bytes 294920 | tf_op jit(solution)/shard_map/ppermute | solution.py:25
  20.9 3.7 %collective-permute-start = (bf16[2,24576]{1,0:T(2,128)(2,1)S(1)}, bf16[2,24576]{1,0:T(2,128)(2,1)S(1)}, u32[]{:S(2)}, u32[]{:S(2)}) collective-permute-start(bf16[2,24576]{1,0:T(2,128)(2,1)S(1)} %convolution_convert_fusion.7), channel_id=1, source_target_pairs={{0,252},{4,0},{8,4},{12,8},{16,12},{20,16},{24,20},{28,24},{32,28}... | collective-permute-start | bytes 294920 | tf_op jit(solution)/shard_map/ppermute | solution.py:25
  25.0 15.1 %copy-start.6 = (bf16[1024,64]{0,1:T(8,128)(2,1)S(1)}, bf16[1024,64]{0,1:T(8,128)(2,1)}, u32[]{:S(2)}) copy-start(bf16[1024,64]{0,1:T(8,128)(2,1)} %param.14) | copy-start | bytes 393220
  44.4 11.1 %copy-start.4 = (bf16[128,1024]{1,0:T(8,128)(2,1)S(1)}, bf16[128,1024]{1,0:T(8,128)(2,1)}, u32[]{:S(2)}) copy-start(bf16[128,1024]{1,0:T(8,128)(2,1)} %param.10) | copy-start | bytes 786436
  44.4 11.1 %copy-start.5 = (bf16[128,1024]{1,0:T(8,128)(2,1)S(1)}, bf16[128,1024]{1,0:T(8,128)(2,1)}, u32[]{:S(2)}) copy-start(bf16[128,1024]{1,0:T(8,128)(2,1)} %param.9) | copy-start | bytes 786436
  44.4 197.1 %all-to-all-start.1 = ((bf16[64,1024,64]{1,2,0:T(8,128)(2,1)}), bf16[64,1024,64]{1,2,0:T(8,128)(2,1)}, u32[]{:S(2)}, u32[]{:S(2)}) async-start(bf16[64,1024,64]{1,2,0:T(8,128)(2,1)} %stack.2), calls=%async_computation.1 | async-start | bytes 16777216 | tf_op jit(solution)/shard_map/all_to_all | solution.py:89
  55.2 35.4 %all-gather.2.cloned.1.call-start = ((), (), s32[]{:S(2)}) async-start(), calls=%async_computation.4 | async-start | bytes 2621440 | tf_op jit(solution)/shard_map/all_gather | solution.py:16
  96.1 1.0 copy-start.2
  241.5 5.1 %copy-start.1 = (bf16[64,8,8,128]{3,2,1,0:T(8,128)(2,1)S(1)}, bf16[64,8,8,128]{3,2,1,0:T(8,128)(2,1)}, u32[]{:S(2)}) copy-start(bf16[64,8,8,128]{3,2,1,0:T(8,128)(2,1)} %copy.59) | copy-start | bytes 3145732
  272.1 3.6 %copy-start.3 = (bf16[2,256,8,128]{1,3,2,0:T(8,128)(2,1)S(1)}, bf16[2,256,8,128]{1,3,2,0:T(8,128)(2,1)}, u32[]{:S(2)}) copy-start(bf16[2,256,8,128]{1,3,2,0:T(8,128)(2,1)} %fusion.12) | copy-start | bytes 3145732
  281.6 18.0 %all-to-all-start.3 = ((bf16[4,512,192]{1,2,0:T(8,128)(2,1)}), bf16[4,512,192]{1,2,0:T(8,128)(2,1)S(1)}, u32[]{:S(2)}, u32[]{:S(2)}) async-start(bf16[4,512,192]{1,2,0:T(8,128)(2,1)} %bitcast.17), calls=%async_computation.3 | async-start | bytes 1572864 | tf_op jit(solution)/shard_map/all_to_all | solution.py:51
  299.6 31.0 %all-to-all-start.2 = ((bf16[4,256,1024]{2,1,0:T(8,128)(2,1)}), bf16[4,256,1024]{2,1,0:T(8,128)(2,1)}, u32[]{:S(2)}, u32[]{:S(2)}) async-start(bf16[4,256,1024]{2,1,0:T(8,128)(2,1)} %bitcast.100), calls=%async_computation.2 | async-start | bytes 4194304 | tf_op jit(solution)/shard_map/all_to_all | solution.py:51
  305.3 6.9 %collective-permute-start.6 = (bf16[2,24576]{1,0:T(2,128)(2,1)S(1)}, bf16[2,24576]{1,0:T(2,128)(2,1)S(1)}, u32[]{:S(2)}, u32[]{:S(2)}) collective-permute-start(bf16[2,24576]{1,0:T(2,128)(2,1)S(1)} %convolution_convert_fusion.1), channel_id=1, source_target_pairs={{0,12},{4,16},{8,20},{12,24},{16,28},{20,32},{24,36},{28,40},{32,4... | collective-permute-start | bytes 294920 | tf_op jit(solution)/shard_map/ppermute | solution.py:25
  307.4 6.8 %collective-permute-start.5 = (bf16[2,24576]{1,0:T(2,128)(2,1)S(1)}, bf16[2,24576]{1,0:T(2,128)(2,1)S(1)}, u32[]{:S(2)}, u32[]{:S(2)}) collective-permute-start(bf16[2,24576]{1,0:T(2,128)(2,1)S(1)} %convolution_convert_fusion.2), channel_id=1, source_target_pairs={{0,8},{4,12},{8,16},{12,20},{16,24},{20,28},{24,32},{28,36},{32,40... | collective-permute-start | bytes 294920 | tf_op jit(solution)/shard_map/ppermute | solution.py:25
  308.7 8.8 %collective-permute-start.7 = (bf16[2,24576]{1,0:T(2,128)(2,1)S(1)}, bf16[2,24576]{1,0:T(2,128)(2,1)S(1)}, u32[]{:S(2)}, u32[]{:S(2)}) collective-permute-start(bf16[2,24576]{1,0:T(2,128)(2,1)S(1)} %convolution_convert_fusion), channel_id=1, source_target_pairs={{0,16},{4,20},{8,24},{12,28},{16,32},{20,36},{24,40},{28,44},{32,4... | collective-permute-start | bytes 294920 | tf_op jit(solution)/shard_map/ppermute | solution.py:25
  310.0 8.6 %collective-permute-start.4 = (bf16[2,24576]{1,0:T(2,128)(2,1)S(1)}, bf16[2,24576]{1,0:T(2,128)(2,1)S(1)}, u32[]{:S(2)}, u32[]{:S(2)}) collective-permute-start(bf16[2,24576]{1,0:T(2,128)(2,1)S(1)} %convolution_convert_fusion.3), channel_id=1, source_target_pairs={{0,4},{4,8},{8,12},{12,16},{16,20},{20,24},{24,28},{28,32},{32,36}... | collective-permute-start | bytes 294920 | tf_op jit(solution)/shard_map/ppermute | solution.py:25
Sparse Core Ops, SparseCore 0:
  57.9 32.6 all-gather.1
